TPU v7x, 512 devices: a whole 4x8x8 slice. The times are simulated.
512 devices in a mesh: face: 16 (over x, z_hi, core), patch: 32 (over z_lo, y).
Axes of the slice: x: 4, y: 8, z: 8 (z_hi: 2, z_lo: 4; z = z_hi * 4 + z_lo), core: 2. Of those that a mesh axis runs over, the one named last changes fastest.
Arguments:
- dust_map: float32 [128, 32768], P('face', 'patch'), may hold values from -12 to 12
- seam_flags: int32 [16, 32, 4], P('face', 'patch'), may hold values from 0 to 1
- block_weights: int32 [128, 4096], P('face', 'patch'), may hold values from 1 to 4
Outputs:
- energy_field: float32 [128, 32768], P('face', 'patch')
- face_moments: float32 [16, 3, 128], P('face')
- sky_moments: float32 [3, 128], replicated
All inputs are finite; a program needn't handle non-finite values.
Results may differ from a plain program's by a relative error of at most 0.0003.
Values sent between devices are 32-bit elements; how exact they have to be, the bound alone decides.
No kernel may reach another device: no remote copies, remote signals or barrier semaphores. Data moves between devices by JAX's collectives and lax.ppermute only.
A program may use at most 64 MiB of HBM per device.

v0:
```python
import math
import jax
import jax.numpy as jnp
import numpy as np
from jax import lax
from jax.sharding import PartitionSpec as P

rim_depth = 4
epsilon = 1e-06
pair_list = ((0, 1), (0, 2), (1, 2))


def extended_2(cells, sides, width):
    for axis, dim in sides:
        count = lax.axis_size(axis)
        head = lax.slice_in_dim(cells, 0, width, axis=dim)
        tail = lax.slice_in_dim(cells, cells.shape[dim] - width, cells.shape[dim], axis=dim)
        cells = jnp.concatenate(
            [
                lax.ppermute(tail, axis, [(i, (i + 1) % count) for i in range(count)]),
                cells,
                lax.ppermute(head, axis, [((i + 1) % count, i) for i in range(count)]),
            ],
            axis=dim,
        )
    return cells


def filter_table():
    shift_rows = np.repeat(np.array([-1.0, 0.0, 1.0]), 3)
    shift_cols = np.tile(np.array([-1.0, 0.0, 1.0]), 3)
    envelope = np.exp(-(shift_rows**2 + shift_cols**2) / 1.28)
    real_rows = []
    imag_rows = []
    for orient in range(8):
        heading = math.pi * orient / 8.0
        phases = 2.2 * (shift_rows * math.cos(heading) + shift_cols * math.sin(heading))
        cosine_part = np.cos(phases) - np.sum(envelope * np.cos(phases)) / np.sum(envelope)
        sine_part = np.sin(phases) - np.sum(envelope * np.sin(phases)) / np.sum(envelope)
        norm_sq = np.sum(envelope**2 * (cosine_part**2 + sine_part**2))
        real_rows.append(envelope * cosine_part / np.sqrt(norm_sq))
        imag_rows.append(envelope * sine_part / np.sqrt(norm_sq))
    return np.stack(real_rows + imag_rows).astype(np.float32)


def turn_rims(extended, seam_bits):
    top_rim = extended[..., :rim_depth, rim_depth:-rim_depth]
    bottom_rim = extended[..., -rim_depth:, rim_depth:-rim_depth]
    left_rim = extended[..., rim_depth:-rim_depth, :rim_depth]
    right_rim = extended[..., rim_depth:-rim_depth, -rim_depth:]
    top_rim = jnp.where(seam_bits[0] > 0, jnp.flip(top_rim, -1), top_rim)
    bottom_rim = jnp.where(seam_bits[1] > 0, jnp.flip(bottom_rim, -1), bottom_rim)
    left_rim = jnp.where(seam_bits[2] > 0, jnp.flip(left_rim, -2), left_rim)
    right_rim = jnp.where(seam_bits[3] > 0, jnp.flip(right_rim, -2), right_rim)
    upper_band = jnp.concatenate(
        [extended[..., :rim_depth, :rim_depth], top_rim, extended[..., :rim_depth, -rim_depth:]],
        axis=-1,
    )
    middle_band = jnp.concatenate(
        [left_rim, extended[..., rim_depth:-rim_depth, rim_depth:-rim_depth], right_rim], axis=-1
    )
    lower_band = jnp.concatenate(
        [
            extended[..., -rim_depth:, :rim_depth],
            bottom_rim,
            extended[..., -rim_depth:, -rim_depth:],
        ],
        axis=-1,
    )
    return jnp.concatenate([upper_band, middle_band, lower_band], axis=-2)


def stencil(extended, dilation, tile_rows, tile_cols, filters):
    pieces = []
    for shift_row in (-1, 0, 1):
        for shift_col in (-1, 0, 1):
            first_row = rim_depth + shift_row * dilation
            first_col = rim_depth + shift_col * dilation
            pieces.append(
                extended[..., first_row : first_row + tile_rows, first_col : first_col + tile_cols]
            )
    stacked = jnp.stack(pieces, 0)
    return jnp.einsum("kt,t...->k...", filters, stacked, precision=lax.Precision.HIGHEST)


def first_layer(extended, tile_rows, tile_cols, filters):
    responses = jnp.stack(
        [stencil(extended, 2**octave, tile_rows, tile_cols, filters) for octave in range(3)]
    )
    moduli = jnp.sqrt(responses[:, :8] ** 2 + responses[:, 8:] ** 2 + epsilon)
    return (responses, moduli)


def second_layer(rimmed, responses, weights, scales, filters, tile_rows, tile_cols):
    moment_rows = []
    energy_parts = []
    for fine_level, coarse_level in pair_list:
        outputs = stencil(
            rimmed[8 * fine_level : 8 * fine_level + 8],
            2**coarse_level,
            tile_rows,
            tile_cols,
            filters,
        )
        outputs = outputs.reshape(2, 8, 8, tile_rows, tile_cols)
        coarse = (responses[coarse_level] * scales[coarse_level]).reshape(
            2, 8, tile_rows, tile_cols
        )
        squares = outputs * outputs
        third_order = jnp.einsum(
            "atrc,atsrc->st", coarse * weights, outputs, precision=lax.Precision.HIGHEST
        )
        fourth_order = jnp.einsum("atsrc,rc->st", squares, weights, precision=lax.Precision.HIGHEST)
        moment_rows.append(jnp.concatenate([third_order.reshape(64), fourth_order.reshape(64)]))
        energy_parts.append(jnp.sum(squares, axis=(0, 1, 2)))
    return (jnp.stack(moment_rows), jnp.stack(energy_parts))


def on_device(dust_map, seam_flags, block_weights):
    tile_rows, tile_cols = dust_map.shape
    filters = jnp.asarray(filter_table())
    seam_bits = seam_flags.reshape(4)
    repeat_by = tile_cols // block_weights.shape[1]
    weights = jnp.repeat(block_weights.astype(jnp.float32), repeat_by, axis=1)
    extended = extended_2(dust_map, (("face", 0), ("patch", 1)), 4)
    extended = turn_rims(extended, seam_bits)
    responses, moduli = first_layer(extended, tile_rows, tile_cols, filters)
    power_terms = jnp.einsum(
        "jtrc,rc->j", moduli * moduli, weights, precision=lax.Precision.HIGHEST
    )
    weight_total = jnp.sum(weights)
    power_sums, weight_sum = lax.psum((power_terms, weight_total), ("face", "patch"))
    levels = power_sums / (8.0 * weight_sum)
    scales = 1.0 / jnp.sqrt(levels)
    fields = (moduli[:2] * scales[:2, None, None, None]).reshape(16, tile_rows, tile_cols)
    rimmed = extended_2(fields, (("face", 1), ("patch", 2)), 4)
    rimmed = turn_rims(rimmed, seam_bits)
    moment_rows, energy_parts = second_layer(
        rimmed, responses, weights, scales, filters, tile_rows, tile_cols
    )
    face_raw, face_weight = lax.psum((moment_rows, weight_total), "patch")
    sky_raw = lax.psum(face_raw, "face")
    face_moments = face_raw / face_weight
    sky_moments = sky_raw / weight_sum
    energy = jnp.sum(energy_parts, 0) / 192.0
    return (energy, face_moments[None], sky_moments)


def solution(mesh):
    return jax.shard_map(
        on_device,
        mesh=mesh,
        in_specs=(P("face", "patch"), P("face", "patch", None), P("face", "patch")),
        out_specs=(P("face", "patch"), P("face", None, None), P()),
        check_vma=False,
    )
```

profile of v0, /device:TPU:1, one launch (start us, length us, event | category | flops | bytes accessed | tf_op | source)
XLA Modules:
  0.0 429.5 jit_solution(8411601705834357442)
XLA Ops:
  1.5 12.0 %collective-permute-start = (f32[4,1024]{1,0:T(4,128)S(1)}, f32[4,1024]{1,0:T(4,128)S(1)}, u32[]{:S(2)}, u32[]{:S(2)}) collective-permute-start(f32[4,1024]{1,0:T(4,128)S(1)} %get-tuple-element.74), channel_id=1, source_target_pairs={{0,32},{32,64},{64,96},{96,128},{128,160},{160,192},{192,224},{224... | collective-permute-start | bytes 49160 | tf_op jit(solution)/shard_map/ppermute | solution.py:20
  13.5 1.9 collective-permute-start.1
  17.0 1.4 fusion.145
  23.3 7.8 %collective-permute-start.3 = (f32[16,4]{1,0:T(8,128)S(1)}, f32[16,4]{1,0:T(8,128)S(1)}, u32[]{:S(2)}, u32[]{:S(2)}) collective-permute-start(f32[16,4]{1,0:T(8,128)S(1)} %get-tuple-element.51), channel_id=1, source_target_pairs={{1,0},{2,1},{3,2},{4,3},{5,4},{6,5},{7,6},{8,7},{9,8},{10,9},{11,1... | collective-permute-start | bytes 776 | tf_op jit(solution)/shard_map/ppermute | solution.py:22
  31.1 1.9 collective-permute-start.2
  34.5 4.9 %collective-permute-done.2 = f32[16,4]{1,0:T(8,128)S(1)} collective-permute-done((f32[16,4]{1,0:T(8,128)S(1)}, f32[16,4]{1,0:T(8,128)S(1)}, u32[]{:S(2)}, u32[]{:S(2)}) %collective-permute-start.2) | collective-permute-done | bytes 288 | tf_op jit(solution)/shard_map/ppermute | solution.py:20
  50.1 1.7 fusion.18
  51.9 1.3 multiply_reduce_fusion.6
  53.9 95.6 %all-reduce = (f32[3]{0:T(128)S(1)}, f32[]{:T(128)}) all-reduce(f32[3]{0:T(128)S(1)} %convolution_bitcast_fusion.1, f32[]{:T(128)} %broadcast_reduce_fusion), channel_id=1, replica_groups=mesh['face'=16,'patch'=32] {'face','patch'}, use_global_device_ids=true, to_apply=%region_1.2 | all-reduce | flops 4 | bytes 32 | tf_op jit(solution)/shard_map/psum | solution.py:132
  150.1 1.2 slice_multiply_fusion.2
  152.7 7.0 %collective-permute-start.4 = (f32[16,4,1024]{2,0,1:T(8,128)}, f32[16,4,1024]{2,0,1:T(8,128)S(1)}, u32[]{:S(2)}, u32[]{:S(2)}) collective-permute-start(f32[16,4,1024]{2,0,1:T(8,128)} %get-tuple-element.42), channel_id=1, source_target_pairs={{0,32},{32,64},{64,96},{96,128},{128,160},{160,192},{192,224},{224... | collective-permute-start | bytes 786440 | tf_op jit(solution)/shard_map/ppermute | solution.py:20
  160.8 1.9 collective-permute-start.5
  163.4 2.6 collective-permute-done.4
  168.6 4.1 collective-permute-done.5
  175.2 5.8 %collective-permute-start.7 = (f32[16,16,4]{2,0,1:T(8,128)S(1)}, f32[16,16,4]{2,0,1:T(8,128)S(1)}, u32[]{:S(2)}, u32[]{:S(2)}) collective-permute-start(f32[16,16,4]{2,0,1:T(8,128)S(1)} %get-tuple-element.18), channel_id=1, source_target_pairs={{1,0},{2,1},{3,2},{4,3},{5,4},{6,5},{7,6},{8,7},{9,8},{10,9},{11,1... | collective-permute-start | bytes 12296 | tf_op jit(solution)/shard_map/ppermute | solution.py:22
  181.0 2.4 fusion.16
  183.4 2.4 collective-permute-start.6
  185.8 8.3 %collective-permute-done.6 = f32[16,16,4]{2,0,1:T(8,128)S(1)} collective-permute-done((f32[16,16,4]{2,0,1:T(8,128)S(1)}, f32[16,16,4]{2,0,1:T(8,128)S(1)}, u32[]{:S(2)}, u32[]{:S(2)}) %collective-permute-start.6) | collective-permute-done | bytes 4128 | tf_op jit(solution)/shard_map/ppermute | solution.py:20
  196.1 1.4 copy-done.1
  204.5 5.5 %multiply_reduce_fusion.4 = (f32[8,1024]{1,0:T(8,128)}, f32[16,8,8,1024]{3,0,2,1:T(8,128)S(1)}) fusion(f32[16,9,1,1]{1,0,3,2:T(8,128)S(1)} %copy-done.12, f32[9,8,8,1024]{3,1,2,0:T(8,128)S(1)} %get-tuple-element.20), kind=kOutput, calls=%fused_computation.16 | convolution fusion | flops 115335168 | bytes 6586944 | tf_op jit(solution)/shard_map/kt,t...->k.../dot_general | solution.py:83
  211.0 11.9 %fusion.2 = f32[8,1,8,1,1]{2,1,4,3,0:T(1,128)S(1)} fusion(f32[2,8,8,8,1024]{4,1,0,3,2:T(8,128)S(1)} %bitcast.261, f32[2,8,8,1024,1]{3,1,0,2,4:T(8,128)S(1)} %copy-done.4), kind=kOutput, calls=%fused_computation.2 | convolution fusion | flops 12582912 | bytes 4718848 | tf_op jit(solution)/shard_map/atrc,atsrc->st/dot_general | solution.py:110
  223.0 13.9 %fusion.147 = f32[1,8,8,1]{1,0,3,2:T(1,128)S(1)} fusion(f32[8,8,8,1024]{3,0,2,1:T(8,128)S(1)} %multiply_reduce_fusion.1, f32[8,1024,1,1]{1,2,0,3:T(1,128)S(1)} %copy-done.9), kind=kOutput, calls=%fused_computation.293 | convolution fusion | flops 6291456 | bytes 2130176 | tf_op jit(solution)/shard_map/atsrc,rc->st/dot_general | solution.py:113
  239.0 6.7 %multiply_reduce_fusion.5 = (f32[8,1024]{1,0:T(8,128)S(1)}, f32[16,8,8,1024]{3,0,2,1:T(8,128)S(1)}) fusion(f32[16,9,1,1]{1,0,3,2:T(8,128)S(1)} %copy-done.12, f32[9,8,8,1024]{3,1,2,0:T(8,128)} %get-tuple-element.26), kind=kOutput, calls=%fused_computation.17 | convolution fusion | flops 115335168 | bytes 6586944 | tf_op jit(solution)/shard_map/kt,t...->k.../dot_general | solution.py:83
  245.7 1.8 multiply_reduce_fusion.2
  247.5 12.1 %fusion.4 = f32[8,1,8,1,1]{2,1,4,3,0:T(1,128)S(1)} fusion(f32[2,8,8,8,1024]{4,1,0,3,2:T(8,128)S(1)} %bitcast.259, f32[2,8,8,1024,1]{3,1,0,2,4:T(8,128)S(1)} %copy-done.7), kind=kOutput, calls=%fused_computation.4 | convolution fusion | flops 12582912 | bytes 4718848 | tf_op jit(solution)/shard_map/atrc,atsrc->st/dot_general | solution.py:110
  259.8 4.8 %multiply_reduce_fusion.3 = (f32[8,1024]{1,0:T(8,128)S(1)}, f32[16,8,8,1024]{3,0,2,1:T(8,128)S(1)}) fusion(f32[16,9,1,1]{1,0,3,2:T(8,128)S(1)} %copy-done.12, f32[9,8,8,1024]{3,1,2,0:T(8,128)S(1)} %copy-done), kind=kOutput, calls=%fused_computation.15 | convolution fusion | flops 115335168 | bytes 6586944 | tf_op jit(solution)/shard_map/kt,t...->k.../dot_general | solution.py:83
  264.6 1.8 multiply_reduce_fusion
  266.4 11.9 %fusion = f32[8,1,8,1,1]{2,1,4,3,0:T(1,128)S(1)} fusion(f32[2,8,8,8,1024]{4,1,0,3,2:T(8,128)S(1)} %bitcast.260, f32[2,8,8,1024,1]{3,1,0,2,4:T(8,128)S(1)} %copy-done.5), kind=kOutput, calls=%fused_computation | convolution fusion | flops 12582912 | bytes 4718848 | tf_op jit(solution)/shard_map/atrc,atsrc->st/dot_general | solution.py:110
  278.4 15.5 %fusion.148 = f32[1,8,8,1]{1,0,3,2:T(1,128)S(1)} fusion(f32[8,8,8,1024]{3,0,2,1:T(8,128)} %multiply_reduce_fusion, f32[8,1024,1,1]{1,2,0,3:T(1,128)S(1)} %copy-done.9), kind=kOutput, calls=%fused_computation.294 | convolution fusion | flops 6291456 | bytes 2130176 | tf_op jit(solution)/shard_map/atsrc,rc->st/dot_general | solution.py:113
  294.0 14.1 %fusion.146 = f32[1,8,8,1]{1,0,3,2:T(1,128)S(1)} fusion(f32[8,8,8,1024]{3,0,2,1:T(8,128)S(1)} %copy-done.3, f32[8,1024,1,1]{1,2,0,3:T(1,128)S(1)} %copy-done.9), kind=kOutput, calls=%fused_computation.292 | convolution fusion | flops 6291456 | bytes 2130176 | tf_op jit(solution)/shard_map/atsrc,rc->st/dot_general | solution.py:113
  308.3 61.2 %all-reduce.1 = (f32[3,128]{1,0:T(4,128)S(1)}, f32[]{:T(128)}) all-reduce(f32[3,128]{1,0:T(4,128)S(1)} %pad_maximum_fusion.12, f32[]{:T(128)} %broadcast_reduce_fusion), channel_id=1, replica_groups=mesh['face'=16,'patch'=32] {'patch'}, use_global_device_ids=true, to_apply=%region_10.11 | all-reduce | flops 385 | bytes 3080 | tf_op jit(solution)/shard_map/psum | solution.py:141
  369.6 56.7 %psum.39 = f32[3,128]{1,0:T(4,128)S(1)} all-reduce(f32[3,128]{1,0:T(4,128)S(1)} %get-tuple-element.14), channel_id=1, replica_groups=mesh['face'=16,'patch'=32] {'face'}, use_global_device_ids=true, to_apply=%region_12.13 | all-reduce | flops 384 | bytes 3072 | tf_op jit(solution)/shard_map/psum | solution.py:142
  (136 shorter events, 41.7 us)
Async XLA Ops:
  0.6 46.1 %copy-start.13 = (f32[16,9,1]{1,0,2:T(8,128)S(1)}, f32[16,9,1]{1,0,2:T(8,128)}, u32[]{:S(2)}) copy-start(f32[16,9,1]{1,0,2:T(8,128)} %constant.23) | copy-start | bytes 1732
  0.6 42.1 %copy-start.6 = (f32[8,1024]{1,0:T(8,128)S(1)}, f32[8,1024]{1,0:T(8,128)}, u32[]{:S(2)}) copy-start(f32[8,1024]{1,0:T(8,128)} %param.4) | copy-start | bytes 98308
  1.5 20.8 %collective-permute-start = (f32[4,1024]{1,0:T(4,128)S(1)}, f32[4,1024]{1,0:T(4,128)S(1)}, u32[]{:S(2)}, u32[]{:S(2)}) collective-permute-start(f32[4,1024]{1,0:T(4,128)S(1)} %get-tuple-element.74), channel_id=1, source_target_pairs={{0,32},{32,64},{64,96},{96,128},{128,160},{160,192},{192,224},{224... | collective-permute-start | bytes 49160 | tf_op jit(solution)/shard_map/ppermute | solution.py:20
  13.5 9.0 %collective-permute-start.1 = (f32[4,1024]{1,0:T(4,128)S(1)}, f32[4,1024]{1,0:T(4,128)S(1)}, u32[]{:S(2)}, u32[]{:S(2)}) collective-permute-start(f32[4,1024]{1,0:T(4,128)S(1)} %get-tuple-element.75), channel_id=1, source_target_pairs={{32,0},{64,32},{96,64},{128,96},{160,128},{192,160},{224,192},{256... | collective-permute-start | bytes 49160 | tf_op jit(solution)/shard_map/ppermute | solution.py:22
  23.3 11.2 %collective-permute-start.3 = (f32[16,4]{1,0:T(8,128)S(1)}, f32[16,4]{1,0:T(8,128)S(1)}, u32[]{:S(2)}, u32[]{:S(2)}) collective-permute-start(f32[16,4]{1,0:T(8,128)S(1)} %get-tuple-element.51), channel_id=1, source_target_pairs={{1,0},{2,1},{3,2},{4,3},{5,4},{6,5},{7,6},{8,7},{9,8},{10,9},{11,1... | collective-permute-start | bytes 776 | tf_op jit(solution)/shard_map/ppermute | solution.py:22
  31.1 8.3 %collective-permute-start.2 = (f32[16,4]{1,0:T(8,128)S(1)}, f32[16,4]{1,0:T(8,128)S(1)}, u32[]{:S(2)}, u32[]{:S(2)}) collective-permute-start(f32[16,4]{1,0:T(8,128)S(1)} %get-tuple-element.52), channel_id=1, source_target_pairs={{0,1},{1,2},{2,3},{3,4},{4,5},{5,6},{6,7},{7,8},{8,9},{9,10},{10,1... | collective-permute-start | bytes 776 | tf_op jit(solution)/shard_map/ppermute | solution.py:20
  152.7 13.2 %collective-permute-start.4 = (f32[16,4,1024]{2,0,1:T(8,128)}, f32[16,4,1024]{2,0,1:T(8,128)S(1)}, u32[]{:S(2)}, u32[]{:S(2)}) collective-permute-start(f32[16,4,1024]{2,0,1:T(8,128)} %get-tuple-element.42), channel_id=1, source_target_pairs={{0,32},{32,64},{64,96},{96,128},{128,160},{160,192},{192,224},{224... | collective-permute-start | bytes 786440 | tf_op jit(solution)/shard_map/ppermute | solution.py:20
  160.8 11.9 %collective-permute-start.5 = (f32[16,4,1024]{2,0,1:T(8,128)}, f32[16,4,1024]{2,0,1:T(8,128)S(1)}, u32[]{:S(2)}, u32[]{:S(2)}) collective-permute-start(f32[16,4,1024]{2,0,1:T(8,128)} %get-tuple-element.41), channel_id=1, source_target_pairs={{32,0},{64,32},{96,64},{128,96},{160,128},{192,160},{224,192},{256... | collective-permute-start | bytes 786440 | tf_op jit(solution)/shard_map/ppermute | solution.py:22
  167.6 1.0 copy-start.10
  174.1 20.4 %copy-start.8 = (f32[16,4,1024]{2,0,1:T(8,128)S(1)}, f32[16,4,1024]{2,0,1:T(8,128)}, u32[]{:S(2)}) copy-start(f32[16,4,1024]{2,0,1:T(8,128)} %get-tuple-element.45) | copy-start | bytes 786436
  175.2 10.5 %collective-permute-start.7 = (f32[16,16,4]{2,0,1:T(8,128)S(1)}, f32[16,16,4]{2,0,1:T(8,128)S(1)}, u32[]{:S(2)}, u32[]{:S(2)}) collective-permute-start(f32[16,16,4]{2,0,1:T(8,128)S(1)} %get-tuple-element.18), channel_id=1, source_target_pairs={{1,0},{2,1},{3,2},{4,3},{5,4},{6,5},{7,6},{8,7},{9,8},{10,9},{11,1... | collective-permute-start | bytes 12296 | tf_op jit(solution)/shard_map/ppermute | solution.py:22
  183.4 10.7 %collective-permute-start.6 = (f32[16,16,4]{2,0,1:T(8,128)S(1)}, f32[16,16,4]{2,0,1:T(8,128)S(1)}, u32[]{:S(2)}, u32[]{:S(2)}) collective-permute-start(f32[16,16,4]{2,0,1:T(8,128)S(1)} %get-tuple-element.19), channel_id=1, source_target_pairs={{0,1},{1,2},{2,3},{3,4},{4,5},{5,6},{6,7},{7,8},{8,9},{9,10},{10,1... | collective-permute-start | bytes 12296 | tf_op jit(solution)/shard_map/ppermute | solution.py:20
  196.1 1.4 copy-start.1
  199.6 3.9 copy-start.2
  200.7 3.8 copy-start.12
  210.0 1.0 copy-start.4
  211.0 12.0 %copy-start.9 = (f32[8,1024,1,1]{1,2,0,3:T(1,128)S(1)}, f32[8,1024,1,1]{1,2,0,3:T(1,128)}, u32[]{:S(2)}) copy-start(f32[8,1024,1,1]{1,2,0,3:T(1,128)} %reshape.101) | copy-start | bytes 98308
  245.7 1.8 copy-start.7
  247.5 12.2 %copy-start = (f32[9,8,8,1024]{3,1,2,0:T(8,128)S(1)}, f32[9,8,8,1024]{3,1,2,0:T(8,128)}, u32[]{:S(2)}) copy-start(f32[9,8,8,1024]{3,1,2,0:T(8,128)} %get-tuple-element.27) | copy-start | bytes 7077892
  264.6 1.8 copy-start.5
  266.4 27.6 %copy-start.3 = (f32[8,8,8,1024]{3,0,2,1:T(8,128)S(1)}, f32[8,8,8,1024]{3,0,2,1:T(8,128)}, u32[]{:S(2)}) copy-start(f32[8,8,8,1024]{3,0,2,1:T(8,128)} %multiply_reduce_fusion.2) | copy-start | bytes 6291460
  278.3 150.3 %copy-start.11 = (f32[8,1024]{1,0:T(8,128)S(1)}, f32[8,1024]{1,0:T(8,128)}, u32[]{:S(2)}) copy-start(f32[8,1024]{1,0:T(8,128)} %get-tuple-element.90) | copy-start | bytes 98308
where the time goes:
time: 437 us; the launch traced here: 429 us
  blocking collectives  214 us (49%)
  matrix products  99.8 us (23%)
  starting transfers between devices  40.7 us (9%)
  other arithmetic  31.7 us (7%)
  waiting for transfers between devices  20.1 us (5%)
  local copies, waits for them, and re-layouts  19.1 us (4%)
  between operations  4.59 us (1%)
    psum x1, blocking collectives, on_device(): lax.psum((power_terms, weight_total), ('face', 'patch'))  95.6 us
    psum x1, blocking collectives, on_device(): face_raw, face_weight = lax.psum((moment_rows, weight_total), 'patch')  61.2 us
    psum x1, blocking collectives, on_device(): sky_raw = lax.psum(face_raw, 'face')  56.7 us
    dot_general x3, matrix products, second_layer(): jnp.einsum('atsrc,rc->st', squares, weights, precision=lax.Precision.HIGH...  43.4 us
    dot_general x3, matrix products, second_layer(): jnp.einsum('atrc,atsrc->st', coarse * weights, outputs, precision=lax.Pre...  35.8 us
    ppermute x4, starting transfers between devices, extended_2(): lax.ppermute(tail, axis, [(i, (i + 1) % count) for i in range(count)])  23.2 us
    dot_general x6, matrix products, stencil(): jnp.einsum('kt,t...->k...', filters, stacked, precision=lax.Precision.HIG...  19.9 us
    ppermute x4, starting transfers between devices, extended_2(): lax.ppermute(head, axis, [((i + 1) % count, i) for i in range(count)])  17.4 us
  transfers between devices with their start and end apart: 8, of which 5 were waited for; matrix products, arithmetic and copies ran while one was open for 3% of the time, Pallas kernels for 0%

commit v1 on v0

--- a/solution.py
+++ b/solution.py
@@ -139,7 +139,7 @@
         rimmed, responses, weights, scales, filters, tile_rows, tile_cols
     )
     face_raw, face_weight = lax.psum((moment_rows, weight_total), "patch")
-    sky_raw = lax.psum(face_raw, "face")
+    sky_raw = jnp.sum(lax.all_gather(face_raw, "face"), axis=0)
     face_moments = face_raw / face_weight
     sky_moments = sky_raw / weight_sum
     energy = jnp.sum(energy_parts, 0) / 192.0

time: 437 us -> 420 us (0.961)
  blocking collectives: 214 us -> 197 us
    psum x1 -> x0, blocking collectives: 56.7 us -> none  [on_device(): sky_raw = lax.psum(face_raw, 'face')]
    all_gather x0 -> x1, blocking collectives: none -> 39.7 us  [on_device(): sky_raw = jnp.sum(lax.all_gather(face_raw, 'face'), axis=0)]
where the time goes in v1:
time: 420 us; the launch traced here: 413 us
  blocking collectives  197 us (47%)
  matrix products  99.8 us (24%)
  starting transfers between devices  40.7 us (10%)
  other arithmetic  31.7 us (8%)
  waiting for transfers between devices  20.1 us (5%)
  local copies, waits for them, and re-layouts  19.1 us (5%)
  between operations  4.59 us (1%)
    psum x1, blocking collectives, on_device(): lax.psum((power_terms, weight_total), ('face', 'patch'))  95.6 us
    psum x1, blocking collectives, on_device(): face_raw, face_weight = lax.psum((moment_rows, weight_total), 'patch')  61.2 us
    dot_general x3, matrix products, second_layer(): jnp.einsum('atsrc,rc->st', squares, weights, precision=lax.Precision.HIGH...  43.4 us
    all_gather x1, blocking collectives, on_device(): sky_raw = jnp.sum(lax.all_gather(face_raw, 'face'), axis=0)  39.7 us
    dot_general x3, matrix products, second_layer(): jnp.einsum('atrc,atsrc->st', coarse * weights, outputs, precision=lax.Pre...  35.8 us
    ppermute x4, starting transfers between devices, extended_2(): lax.ppermute(tail, axis, [(i, (i + 1) % count) for i in range(count)])  23.2 us
    dot_general x6, matrix products, stencil(): jnp.einsum('kt,t...->k...', filters, stacked, precision=lax.Precision.HIG...  19.9 us
    ppermute x4, starting transfers between devices, extended_2(): lax.ppermute(head, axis, [((i + 1) % count, i) for i in range(count)])  17.4 us
  transfers between devices with their start and end apart: 8, of which 5 were waited for; matrix products, arithmetic and copies ran while one was open for 3% of the time, Pallas kernels for 0%

profile of v1, /device:TPU:1, one launch (start us, length us, event | category | flops | bytes accessed | tf_op | source)
XLA Modules:
  0.0 412.5 jit_solution(585193986728215941)
XLA Ops:
  1.5 12.0 %collective-permute-start = (f32[4,1024]{1,0:T(4,128)S(1)}, f32[4,1024]{1,0:T(4,128)S(1)}, u32[]{:S(2)}, u32[]{:S(2)}) collective-permute-start(f32[4,1024]{1,0:T(4,128)S(1)} %get-tuple-element.74), channel_id=1, source_target_pairs={{0,32},{32,64},{64,96},{96,128},{128,160},{160,192},{192,224},{224... | collective-permute-start | bytes 49160 | tf_op jit(solution)/shard_map/ppermute | solution.py:20
  13.5 1.9 collective-permute-start.1
  17.0 1.4 fusion.145
  23.3 7.8 %collective-permute-start.3 = (f32[16,4]{1,0:T(8,128)S(1)}, f32[16,4]{1,0:T(8,128)S(1)}, u32[]{:S(2)}, u32[]{:S(2)}) collective-permute-start(f32[16,4]{1,0:T(8,128)S(1)} %get-tuple-element.51), channel_id=1, source_target_pairs={{1,0},{2,1},{3,2},{4,3},{5,4},{6,5},{7,6},{8,7},{9,8},{10,9},{11,1... | collective-permute-start | bytes 776 | tf_op jit(solution)/shard_map/ppermute | solution.py:22
  31.1 1.9 collective-permute-start.2
  34.5 4.9 %collective-permute-done.2 = f32[16,4]{1,0:T(8,128)S(1)} collective-permute-done((f32[16,4]{1,0:T(8,128)S(1)}, f32[16,4]{1,0:T(8,128)S(1)}, u32[]{:S(2)}, u32[]{:S(2)}) %collective-permute-start.2) | collective-permute-done | bytes 288 | tf_op jit(solution)/shard_map/ppermute | solution.py:20
  50.1 1.7 fusion.18
  51.9 1.3 multiply_reduce_fusion.6
  53.9 95.6 %all-reduce = (f32[3]{0:T(128)S(1)}, f32[]{:T(128)}) all-reduce(f32[3]{0:T(128)S(1)} %convolution_bitcast_fusion.1, f32[]{:T(128)} %broadcast_reduce_fusion), channel_id=1, replica_groups=mesh['face'=16,'patch'=32] {'face','patch'}, use_global_device_ids=true, to_apply=%region_1.2 | all-reduce | flops 4 | bytes 32 | tf_op jit(solution)/shard_map/psum | solution.py:132
  150.1 1.2 slice_multiply_fusion.2
  152.7 7.0 %collective-permute-start.4 = (f32[16,4,1024]{2,0,1:T(8,128)}, f32[16,4,1024]{2,0,1:T(8,128)S(1)}, u32[]{:S(2)}, u32[]{:S(2)}) collective-permute-start(f32[16,4,1024]{2,0,1:T(8,128)} %get-tuple-element.42), channel_id=1, source_target_pairs={{0,32},{32,64},{64,96},{96,128},{128,160},{160,192},{192,224},{224... | collective-permute-start | bytes 786440 | tf_op jit(solution)/shard_map/ppermute | solution.py:20
  160.8 1.9 collective-permute-start.5
  163.4 2.6 collective-permute-done.4
  168.6 4.1 collective-permute-done.5
  175.2 5.8 %collective-permute-start.7 = (f32[16,16,4]{2,0,1:T(8,128)S(1)}, f32[16,16,4]{2,0,1:T(8,128)S(1)}, u32[]{:S(2)}, u32[]{:S(2)}) collective-permute-start(f32[16,16,4]{2,0,1:T(8,128)S(1)} %get-tuple-element.18), channel_id=1, source_target_pairs={{1,0},{2,1},{3,2},{4,3},{5,4},{6,5},{7,6},{8,7},{9,8},{10,9},{11,1... | collective-permute-start | bytes 12296 | tf_op jit(solution)/shard_map/ppermute | solution.py:22
  181.0 2.4 fusion.16
  183.4 2.4 collective-permute-start.6
  185.8 8.3 %collective-permute-done.6 = f32[16,16,4]{2,0,1:T(8,128)S(1)} collective-permute-done((f32[16,16,4]{2,0,1:T(8,128)S(1)}, f32[16,16,4]{2,0,1:T(8,128)S(1)}, u32[]{:S(2)}, u32[]{:S(2)}) %collective-permute-start.6) | collective-permute-done | bytes 4128 | tf_op jit(solution)/shard_map/ppermute | solution.py:20
  196.1 1.4 copy-done.1
  204.5 5.5 %multiply_reduce_fusion.4 = (f32[8,1024]{1,0:T(8,128)}, f32[16,8,8,1024]{3,0,2,1:T(8,128)S(1)}) fusion(f32[16,9,1,1]{1,0,3,2:T(8,128)S(1)} %copy-done.12, f32[9,8,8,1024]{3,1,2,0:T(8,128)S(1)} %get-tuple-element.20), kind=kOutput, calls=%fused_computation.16 | convolution fusion | flops 115335168 | bytes 6586944 | tf_op jit(solution)/shard_map/kt,t...->k.../dot_general | solution.py:83
  211.0 11.9 %fusion.2 = f32[8,1,8,1,1]{2,1,4,3,0:T(1,128)S(1)} fusion(f32[2,8,8,8,1024]{4,1,0,3,2:T(8,128)S(1)} %bitcast.262, f32[2,8,8,1024,1]{3,1,0,2,4:T(8,128)S(1)} %copy-done.4), kind=kOutput, calls=%fused_computation.2 | convolution fusion | flops 12582912 | bytes 4718848 | tf_op jit(solution)/shard_map/atrc,atsrc->st/dot_general | solution.py:110
  223.0 13.9 %fusion.147 = f32[1,8,8,1]{1,0,3,2:T(1,128)S(1)} fusion(f32[8,8,8,1024]{3,0,2,1:T(8,128)S(1)} %multiply_reduce_fusion.1, f32[8,1024,1,1]{1,2,0,3:T(1,128)S(1)} %copy-done.9), kind=kOutput, calls=%fused_computation.293 | convolution fusion | flops 6291456 | bytes 2130176 | tf_op jit(solution)/shard_map/atsrc,rc->st/dot_general | solution.py:113
  239.0 6.7 %multiply_reduce_fusion.5 = (f32[8,1024]{1,0:T(8,128)S(1)}, f32[16,8,8,1024]{3,0,2,1:T(8,128)S(1)}) fusion(f32[16,9,1,1]{1,0,3,2:T(8,128)S(1)} %copy-done.12, f32[9,8,8,1024]{3,1,2,0:T(8,128)} %get-tuple-element.26), kind=kOutput, calls=%fused_computation.17 | convolution fusion | flops 115335168 | bytes 6586944 | tf_op jit(solution)/shard_map/kt,t...->k.../dot_general | solution.py:83
  245.7 1.8 multiply_reduce_fusion.2
  247.5 12.1 %fusion.4 = f32[8,1,8,1,1]{2,1,4,3,0:T(1,128)S(1)} fusion(f32[2,8,8,8,1024]{4,1,0,3,2:T(8,128)S(1)} %bitcast.260, f32[2,8,8,1024,1]{3,1,0,2,4:T(8,128)S(1)} %copy-done.7), kind=kOutput, calls=%fused_computation.4 | convolution fusion | flops 12582912 | bytes 4718848 | tf_op jit(solution)/shard_map/atrc,atsrc->st/dot_general | solution.py:110
  259.8 4.8 %multiply_reduce_fusion.3 = (f32[8,1024]{1,0:T(8,128)S(1)}, f32[16,8,8,1024]{3,0,2,1:T(8,128)S(1)}) fusion(f32[16,9,1,1]{1,0,3,2:T(8,128)S(1)} %copy-done.12, f32[9,8,8,1024]{3,1,2,0:T(8,128)S(1)} %copy-done), kind=kOutput, calls=%fused_computation.15 | convolution fusion | flops 115335168 | bytes 6586944 | tf_op jit(solution)/shard_map/kt,t...->k.../dot_general | solution.py:83
  264.6 1.8 multiply_reduce_fusion
  266.4 11.9 %fusion = f32[8,1,8,1,1]{2,1,4,3,0:T(1,128)S(1)} fusion(f32[2,8,8,8,1024]{4,1,0,3,2:T(8,128)S(1)} %bitcast.261, f32[2,8,8,1024,1]{3,1,0,2,4:T(8,128)S(1)} %copy-done.5), kind=kOutput, calls=%fused_computation | convolution fusion | flops 12582912 | bytes 4718848 | tf_op jit(solution)/shard_map/atrc,atsrc->st/dot_general | solution.py:110
  278.4 15.5 %fusion.148 = f32[1,8,8,1]{1,0,3,2:T(1,128)S(1)} fusion(f32[8,8,8,1024]{3,0,2,1:T(8,128)} %multiply_reduce_fusion, f32[8,1024,1,1]{1,2,0,3:T(1,128)S(1)} %copy-done.9), kind=kOutput, calls=%fused_computation.294 | convolution fusion | flops 6291456 | bytes 2130176 | tf_op jit(solution)/shard_map/atsrc,rc->st/dot_general | solution.py:113
  294.0 14.1 %fusion.146 = f32[1,8,8,1]{1,0,3,2:T(1,128)S(1)} fusion(f32[8,8,8,1024]{3,0,2,1:T(8,128)S(1)} %copy-done.3, f32[8,1024,1,1]{1,2,0,3:T(1,128)S(1)} %copy-done.9), kind=kOutput, calls=%fused_computation.292 | convolution fusion | flops 6291456 | bytes 2130176 | tf_op jit(solution)/shard_map/atsrc,rc->st/dot_general | solution.py:113
  308.3 61.2 %all-reduce.1 = (f32[3,128]{1,0:T(4,128)S(1)}, f32[]{:T(128)}) all-reduce(f32[3,128]{1,0:T(4,128)S(1)} %pad_maximum_fusion.12, f32[]{:T(128)} %broadcast_reduce_fusion), channel_id=1, replica_groups=mesh['face'=16,'patch'=32] {'patch'}, use_global_device_ids=true, to_apply=%region_10.11 | all-reduce | flops 385 | bytes 3080 | tf_op jit(solution)/shard_map/psum | solution.py:141
  370.8 39.7 %all-gather.1 = f32[16,3,128]{2,1,0:T(4,128)S(1)} all-gather(f32[1,3,128]{2,1,0:T(4,128)S(1)} %bitcast.274), channel_id=2, replica_groups=mesh['face'=16,'patch'=32] {'face'}, dimensions={0}, use_global_device_ids=true | all-gather | bytes 26112 | tf_op jit(solution)/shard_map/all_gather | solution.py:142
  (137 shorter events, 41.7 us)
Async XLA Ops:
  0.6 46.1 %copy-start.13 = (f32[16,9,1]{1,0,2:T(8,128)S(1)}, f32[16,9,1]{1,0,2:T(8,128)}, u32[]{:S(2)}) copy-start(f32[16,9,1]{1,0,2:T(8,128)} %constant.23) | copy-start | bytes 1732
  0.6 42.1 %copy-start.6 = (f32[8,1024]{1,0:T(8,128)S(1)}, f32[8,1024]{1,0:T(8,128)}, u32[]{:S(2)}) copy-start(f32[8,1024]{1,0:T(8,128)} %param.4) | copy-start | bytes 98308
  1.5 20.8 %collective-permute-start = (f32[4,1024]{1,0:T(4,128)S(1)}, f32[4,1024]{1,0:T(4,128)S(1)}, u32[]{:S(2)}, u32[]{:S(2)}) collective-permute-start(f32[4,1024]{1,0:T(4,128)S(1)} %get-tuple-element.74), channel_id=1, source_target_pairs={{0,32},{32,64},{64,96},{96,128},{128,160},{160,192},{192,224},{224... | collective-permute-start | bytes 49160 | tf_op jit(solution)/shard_map/ppermute | solution.py:20
  13.5 9.0 %collective-permute-start.1 = (f32[4,1024]{1,0:T(4,128)S(1)}, f32[4,1024]{1,0:T(4,128)S(1)}, u32[]{:S(2)}, u32[]{:S(2)}) collective-permute-start(f32[4,1024]{1,0:T(4,128)S(1)} %get-tuple-element.75), channel_id=1, source_target_pairs={{32,0},{64,32},{96,64},{128,96},{160,128},{192,160},{224,192},{256... | collective-permute-start | bytes 49160 | tf_op jit(solution)/shard_map/ppermute | solution.py:22
  23.3 11.2 %collective-permute-start.3 = (f32[16,4]{1,0:T(8,128)S(1)}, f32[16,4]{1,0:T(8,128)S(1)}, u32[]{:S(2)}, u32[]{:S(2)}) collective-permute-start(f32[16,4]{1,0:T(8,128)S(1)} %get-tuple-element.51), channel_id=1, source_target_pairs={{1,0},{2,1},{3,2},{4,3},{5,4},{6,5},{7,6},{8,7},{9,8},{10,9},{11,1... | collective-permute-start | bytes 776 | tf_op jit(solution)/shard_map/ppermute | solution.py:22
  31.1 8.3 %collective-permute-start.2 = (f32[16,4]{1,0:T(8,128)S(1)}, f32[16,4]{1,0:T(8,128)S(1)}, u32[]{:S(2)}, u32[]{:S(2)}) collective-permute-start(f32[16,4]{1,0:T(8,128)S(1)} %get-tuple-element.52), channel_id=1, source_target_pairs={{0,1},{1,2},{2,3},{3,4},{4,5},{5,6},{6,7},{7,8},{8,9},{9,10},{10,1... | collective-permute-start | bytes 776 | tf_op jit(solution)/shard_map/ppermute | solution.py:20
  152.7 13.2 %collective-permute-start.4 = (f32[16,4,1024]{2,0,1:T(8,128)}, f32[16,4,1024]{2,0,1:T(8,128)S(1)}, u32[]{:S(2)}, u32[]{:S(2)}) collective-permute-start(f32[16,4,1024]{2,0,1:T(8,128)} %get-tuple-element.42), channel_id=1, source_target_pairs={{0,32},{32,64},{64,96},{96,128},{128,160},{160,192},{192,224},{224... | collective-permute-start | bytes 786440 | tf_op jit(solution)/shard_map/ppermute | solution.py:20
  160.8 11.9 %collective-permute-start.5 = (f32[16,4,1024]{2,0,1:T(8,128)}, f32[16,4,1024]{2,0,1:T(8,128)S(1)}, u32[]{:S(2)}, u32[]{:S(2)}) collective-permute-start(f32[16,4,1024]{2,0,1:T(8,128)} %get-tuple-element.41), channel_id=1, source_target_pairs={{32,0},{64,32},{96,64},{128,96},{160,128},{192,160},{224,192},{256... | collective-permute-start | bytes 786440 | tf_op jit(solution)/shard_map/ppermute | solution.py:22
  167.6 1.0 copy-start.10
  174.1 20.4 %copy-start.8 = (f32[16,4,1024]{2,0,1:T(8,128)S(1)}, f32[16,4,1024]{2,0,1:T(8,128)}, u32[]{:S(2)}) copy-start(f32[16,4,1024]{2,0,1:T(8,128)} %get-tuple-element.45) | copy-start | bytes 786436
  175.2 10.5 %collective-permute-start.7 = (f32[16,16,4]{2,0,1:T(8,128)S(1)}, f32[16,16,4]{2,0,1:T(8,128)S(1)}, u32[]{:S(2)}, u32[]{:S(2)}) collective-permute-start(f32[16,16,4]{2,0,1:T(8,128)S(1)} %get-tuple-element.18), channel_id=1, source_target_pairs={{1,0},{2,1},{3,2},{4,3},{5,4},{6,5},{7,6},{8,7},{9,8},{10,9},{11,1... | collective-permute-start | bytes 12296 | tf_op jit(solution)/shard_map/ppermute | solution.py:22
  183.4 10.7 %collective-permute-start.6 = (f32[16,16,4]{2,0,1:T(8,128)S(1)}, f32[16,16,4]{2,0,1:T(8,128)S(1)}, u32[]{:S(2)}, u32[]{:S(2)}) collective-permute-start(f32[16,16,4]{2,0,1:T(8,128)S(1)} %get-tuple-element.19), channel_id=1, source_target_pairs={{0,1},{1,2},{2,3},{3,4},{4,5},{5,6},{6,7},{7,8},{8,9},{9,10},{10,1... | collective-permute-start | bytes 12296 | tf_op jit(solution)/shard_map/ppermute | solution.py:20
  196.1 1.4 copy-start.1
  199.6 3.9 copy-start.2
  200.7 3.8 copy-start.12
  210.0 1.0 copy-start.4
  211.0 12.0 %copy-start.9 = (f32[8,1024,1,1]{1,2,0,3:T(1,128)S(1)}, f32[8,1024,1,1]{1,2,0,3:T(1,128)}, u32[]{:S(2)}) copy-start(f32[8,1024,1,1]{1,2,0,3:T(1,128)} %reshape.105) | copy-start | bytes 98308
  245.7 1.8 copy-start.7
  247.5 12.2 %copy-start = (f32[9,8,8,1024]{3,1,2,0:T(8,128)S(1)}, f32[9,8,8,1024]{3,1,2,0:T(8,128)}, u32[]{:S(2)}) copy-start(f32[9,8,8,1024]{3,1,2,0:T(8,128)} %get-tuple-element.27) | copy-start | bytes 7077892
  264.6 1.8 copy-start.5
  266.4 27.6 %copy-start.3 = (f32[8,8,8,1024]{3,0,2,1:T(8,128)S(1)}, f32[8,8,8,1024]{3,0,2,1:T(8,128)}, u32[]{:S(2)}) copy-start(f32[8,8,8,1024]{3,0,2,1:T(8,128)} %multiply_reduce_fusion.2) | copy-start | bytes 6291460
  278.3 133.4 %copy-start.11 = (f32[8,1024]{1,0:T(8,128)S(1)}, f32[8,1024]{1,0:T(8,128)}, u32[]{:S(2)}) copy-start(f32[8,1024]{1,0:T(8,128)} %get-tuple-element.90) | copy-start | bytes 98308
